TPU v7x, 32 devices: a whole 2x2x4 slice. The times are simulated.
32 devices in a mesh: recon: 1, slab: 32 (over z, y, x, core), coil: 1.
Axes of the slice: x: 2, y: 2, z: 4, core: 2. Of those that a mesh axis runs over, the one named last changes fastest.
Arguments:
- image: float32 [2, 192, 192, 192], P('recon', 'slab'), may hold values from -6 to 6
- prox_point: float32 [2, 192, 192, 192], P('recon', 'slab'), may hold values from -6 to 6
- dual: float32 [2, 192, 192, 192], P('recon', 'slab'), may hold values from -6 to 6
- adjoint_data: float32 [2, 192, 192, 192], P('recon', 'slab'), may hold values from -6 to 6
- coil_maps: float32 [1, 2, 192, 192, 192], P('coil', 'recon', 'slab'), may hold values from -4 to 4
- kernel: float32 [384, 384, 384], P('slab'), may hold values from 0.05 to 5
Outputs:
- image_new: float32 [2, 192, 192, 192], P('recon', 'slab')
- prox_new: float32 [2, 192, 192, 192], P('recon', 'slab')
- dual_new: float32 [2, 192, 192, 192], P('recon', 'slab')
All inputs are finite; a program needn't handle non-finite values.
Results may differ from a plain program's by a relative error of at most 0.00015.
Values sent between devices are 32-bit elements; how exact they have to be, the bound alone decides.
A program may use at most 192 MiB of HBM per device.

v0:
```python
import math

import jax
import jax.numpy as jnp
from jax import lax
from jax.sharding import PartitionSpec as P

half_root = 0.7071067811865476
shrink = 0.5
step_size = 0.25
penalty = 1.0


def extended_2(cells, sides, width):
    for axis, dim in sides:
        count = lax.axis_size(axis)
        head = lax.slice_in_dim(cells, 0, width, axis=dim)
        tail = lax.slice_in_dim(cells, cells.shape[dim] - width, cells.shape[dim], axis=dim)
        cells = jnp.concatenate(
            [
                lax.ppermute(tail, axis, [(i, (i + 1) % count) for i in range(count)]),
                cells,
                lax.ppermute(head, axis, [((i + 1) % count, i) for i in range(count)]),
            ],
            axis=dim,
        )
    return cells


def complex_table(angle):
    cosine = jnp.cos(angle)
    sine = jnp.sin(angle)
    return jnp.stack([jnp.stack([cosine, sine]), jnp.stack([-sine, cosine])])


def spectral(parts, length, out_length, direction, trailing):
    highest = lax.Precision.HIGHEST
    inner_len = length // 16
    shape = parts.shape
    axis_dim = parts.ndim - 1 - trailing
    rows_in = shape[axis_dim] // inner_len
    tail = shape[axis_dim + 1 :]
    parts = parts.reshape(shape[:axis_dim] + (rows_in, inner_len) + tail)
    letters = "uv"[:trailing]
    index_n = jnp.arange(rows_in)[:, None]
    index_k = jnp.arange(16)[None, :]
    angle_one = direction * 2.0 * math.pi / 16 * (index_n * index_k % 16).astype(jnp.float32)
    parts = jnp.einsum(
        "p...nq" + letters + ",prnk->r...kq" + letters,
        parts,
        complex_table(angle_one),
        precision=highest,
    )
    index_q = jnp.arange(inner_len)
    angle_two = (
        direction
        * 2.0
        * math.pi
        / length
        * (jnp.arange(16)[:, None] * index_q[None, :] % length).astype(jnp.float32)
    )
    angle_two = angle_two.reshape((16, inner_len) + (1,) * trailing)
    cos_two = jnp.cos(angle_two)
    sin_two = jnp.sin(angle_two)
    twisted = jnp.stack(
        [parts[0] * cos_two - parts[1] * sin_two, parts[0] * sin_two + parts[1] * cos_two]
    )
    columns = out_length // 16
    angle_three = (
        direction
        * 2.0
        * math.pi
        / inner_len
        * (index_q[:, None] * jnp.arange(columns)[None, :] % inner_len).astype(jnp.float32)
    )
    parts = jnp.einsum(
        "p...kq" + letters + ",prqm->r...mk" + letters,
        twisted,
        complex_table(angle_three),
        precision=highest,
    )
    return parts.reshape(shape[:axis_dim] + (out_length,) + tail)


def pair_local(values, axis_dim, offset):
    length = values.shape[axis_dim]
    layout = [1] * values.ndim
    layout[axis_dim] = length
    is_first = ((jnp.arange(length) - offset) % 2 == 0).reshape(layout)
    after_one = jnp.roll(values, -1, axis_dim)
    before_one = jnp.roll(values, 1, axis_dim)
    return jnp.where(is_first, (values + after_one) * half_root, (before_one - values) * half_root)


def pair_planes(extended, own_first):
    middle = extended[:, 1:-1]
    after_one = extended[:, 2:]
    before_one = extended[:, :-2]
    marked = own_first[None, :, None, None]
    return jnp.where(marked, (middle + after_one) * half_root, (before_one - middle) * half_root)


def spin(extended, base, offset):
    total_planes = extended.shape[1]
    global_plane = base - 1 + jnp.arange(total_planes, dtype=jnp.int32)
    plane_first = (global_plane - offset) % 2 == 0
    own_first = plane_first[1:-1]
    lower_rim = (extended[:, :1] + extended[:, 1:2]) * half_root
    upper_rim = (extended[:, -2:-1] - extended[:, -1:]) * half_root
    coefs = jnp.concatenate([lower_rim, pair_planes(extended, own_first), upper_rim], axis=1)
    coefs = pair_local(coefs, 2, offset)
    coefs = pair_local(coefs, 3, offset)
    rows_first = (jnp.arange(extended.shape[2]) - offset) % 2 == 0
    cols_first = (jnp.arange(extended.shape[3]) - offset) % 2 == 0
    keep = plane_first[:, None, None] & rows_first[None, :, None] & cols_first[None, None, :]
    magnitude = jnp.sqrt(coefs[0] * coefs[0] + coefs[1] * coefs[1])
    factor = jnp.maximum(magnitude - shrink, 0.0) / jnp.maximum(magnitude, shrink)
    coefs = jnp.where(keep[None], coefs, coefs * factor[None])
    coefs = pair_local(coefs, 3, offset)
    coefs = pair_local(coefs, 2, offset)
    return pair_planes(coefs, own_first)


def on_device(image, prox_point, dual, adjoint_data, coil_maps, kernel):
    grid_len = kernel.shape[1]
    image_width = image.shape[3]
    sens_real = coil_maps[:, 0]
    sens_imag = coil_maps[:, 1]
    coil_field = jnp.stack(
        [sens_real * image[0] - sens_imag * image[1], sens_real * image[1] + sens_imag * image[0]]
    )
    coil_field = spectral(coil_field, grid_len, grid_len, -1.0, 1)
    gain_zyx = jnp.transpose(kernel, (2, 0, 1))
    piece = lax.all_to_all(coil_field, "slab", split_axis=3, concat_axis=2, tiled=True)
    piece = spectral(piece, grid_len, grid_len, -1.0, 0)
    piece = spectral(piece, grid_len, grid_len, -1.0, 2)
    piece = piece * gain_zyx
    piece = spectral(piece, grid_len, image_width, 1.0, 2)
    piece = spectral(piece, grid_len, image_width, 1.0, 0)
    back = lax.all_to_all(piece, "slab", split_axis=2, concat_axis=3, tiled=True)
    back = spectral(back, grid_len, image_width, 1.0, 1)
    scale = 1.0 / float(grid_len * grid_len * grid_len)
    local_real = jnp.sum(sens_real * back[0] + sens_imag * back[1], axis=0) * scale
    local_imag = jnp.sum(sens_real * back[1] - sens_imag * back[0], axis=0) * scale
    normal_real, normal_imag = lax.psum((local_real, local_imag), "coil")
    normal = jnp.stack([normal_real, normal_imag])
    image_new = image - step_size * (normal - adjoint_data + penalty * (image - prox_point + dual))
    merged = image_new + dual
    extended = extended_2(merged, (("slab", 1),), 1)
    planes = merged.shape[1]
    base = lax.axis_index("slab") * planes
    prox_new = 0.5 * (spin(extended, base, 0) + spin(extended, base, 1))
    dual_new = dual + image_new - prox_new
    return (image_new, prox_new, dual_new)


def solution(mesh):
    in_specs = (
        P("recon", "slab", None, None),
        P("recon", "slab", None, None),
        P("recon", "slab", None, None),
        P("recon", "slab", None, None),
        P("coil", "recon", "slab", None, None),
        P("slab", None, None),
    )
    out_specs = (
        P("recon", "slab", None, None),
        P("recon", "slab", None, None),
        P("recon", "slab", None, None),
    )
    return jax.shard_map(
        on_device, mesh=mesh, in_specs=in_specs, out_specs=out_specs, check_vma=False
    )
```

profile of v0, /device:TPU:0, one launch (start us, length us, event | category | flops | bytes accessed | tf_op | source)
XLA Modules:
  0.0 693.3 jit_solution(12385043103243765433)
XLA Ops:
  1.0 2.6 fusion.112
  4.4 4.0 fusion.96
  9.8 7.3 %fusion.97 = f32[2,1,6,24,16,192]{5,3,4,2,0,1:T(8,128)S(1)} fusion(f32[2,6,16,24,192]{4,2,3,1,0:T(8,128)S(1)} %maximum_bitcast_fusion.4, f32[1,2,24,24]{2,3,0,1:T(8,128)S(1)} %get-tuple-element.68, f32[1,2,24,24]{2,3,0,1:T(8,128)S(1)} %get-tuple-element.67), kind=kOutput, calls=%fused_computation.130 | convolution fusion | flops 509610240 | bytes 7087104 | tf_op jit(solution)/shard_map/p...kqu,prqm->r...mku/dot_general | solution.py:76
  18.5 5.8 copy.116
  24.3 7.6 %all-to-all-start = ((f32[2,1,6,384,192]{4,0,2,1,3:T(2,128)}), f32[2,1,6,384,192]{4,0,2,1,3:T(2,128)}, u32[]{:S(2)}, u32[]{:S(2)}) async-start(f32[2,1,6,384,192]{4,0,2,1,3:T(2,128)} %copy.116), calls=%async_computation | async-start | bytes 9437184 | tf_op jit(solution)/shard_map/all_to_all | solution.py:134
  31.9 8.1 %copy.125 = f32[12,384,384]{1,2,0:T(8,128)} copy(f32[12,384,384]{2,1,0:T(8,128)} %param.11) | data formatting | bytes 14155776 | tf_op args[5]
  40.4 96.6 %all-to-all-done = f32[2,1,6,384,192]{4,0,2,1,3:T(2,128)} async-done(((f32[2,1,6,384,192]{4,0,2,1,3:T(2,128)}), f32[2,1,6,384,192]{4,0,2,1,3:T(2,128)}, u32[]{:S(2)}, u32[]{:S(2)}) %all-to-all-start) | async-done | bytes 3538976 | tf_op jit(solution)/shard_map/all_to_all | solution.py:134
  137.0 4.0 copy.117
  140.9 5.1 copy.118
  146.0 14.6 %reshape.987 = f32[2,192,12,8,24]{4,3,0,2,1:T(8,128)} reshape(f32[2,1,32,6,12,192]{5,0,4,3,2,1:T(2,128)} %copy.118) | data formatting | bytes 7077888 | tf_op jit(solution)/shard_map/reshape.9
  160.6 13.2 %copy.119 = f32[2,192,12,8,24]{1,3,0,4,2:T(8,128)} copy(f32[2,192,12,8,24]{4,3,0,2,1:T(8,128)} %reshape.987) | data formatting | bytes 7077888 | tf_op jit(solution)/shard_map/reshape.9
  173.9 9.7 %fusion.48 = f32[2,1,192,12,16,24]{2,4,5,3,0,1:T(8,128)S(1)} fusion(f32[2,192,12,8,24]{1,3,0,4,2:T(8,128)} %copy.119, f32[1,2,8,16]{3,2,0,1:T(8,128)S(1)} %get-tuple-element.74, f32[1,2,8,16]{3,2,0,1:T(8,128)S(1)} %get-tuple-element.73), kind=kOutput, calls=%fused_computation.57 | convolution fusion | flops 339739136 | bytes 10618880 | tf_op jit(solution)/shard_map/p...nq,prnk->r...kq/dot_general | solution.py:48
  183.5 1.9 multiply_subtract_fusion.1
  187.2 14.4 %fusion.42 = f32[2,1,192,12,24,16]{2,4,5,3,0,1:T(8,128)S(1)} fusion(f32[2,192,12,16,24]{1,3,4,2,0:T(8,128)S(1)} %maximum_bitcast_fusion.2, f32[1,2,24,24]{2,3,0,1:T(8,128)S(1)} %get-tuple-element.68, f32[1,2,24,24]{2,3,0,1:T(8,128)S(1)} %get-tuple-element.67), kind=kOutput, calls=%fused_computation.55 | convolution fusion | flops 1019218176 | bytes 14164992 | tf_op jit(solution)/shard_map/p...kq,prqm->r...mk/dot_general | solution.py:76
  201.6 7.2 %copy.121 = f32[2,1,192,12,24,16]{2,5,4,3,0,1:T(8,128)} copy(f32[2,1,192,12,24,16]{2,4,5,3,0,1:T(8,128)S(1)} %fusion.42) | data formatting | bytes 14155776 | tf_op jit(solution)/shard_map/p...kq,prqm->r...mk/transpose | solution.py:76
  208.8 24.5 %reshape.989 = f32[2,8,24,12,384]{2,1,4,3,0:T(8,128)} reshape(f32[2,1,192,12,24,16]{2,5,4,3,0,1:T(8,128)} %copy.121) | data formatting | bytes 14155776 | tf_op jit(solution)/shard_map/reshape.17
  233.3 24.9 %copy.122 = f32[2,8,24,12,384]{4,1,0,3,2:T(8,128)} copy(f32[2,8,24,12,384]{2,1,4,3,0:T(8,128)} %reshape.989) | data formatting | bytes 14155776 | tf_op jit(solution)/shard_map/reshape.17
  258.1 13.9 %fusion.19 = f32[2,16,24,12,384]{4,1,3,2,0:T(8,128)S(1)} fusion(f32[2,8,24,12,384]{4,1,0,3,2:T(8,128)} %copy.122, f32[2,2,8,16,1,1]{3,2,0,5,4,1:T(8,128)S(1)} %maximum_bitcast_fusion.36), kind=kOutput, calls=%fused_computation.28 | convolution fusion | flops 679477248 | bytes 21235712 | tf_op jit(solution)/shard_map/p...nquv,prnk->r...kquv/dot_general | solution.py:48
  272.0 6.1 subtract_bitcast_fusion.1
  278.1 11.7 %maximum_bitcast_fusion = f32[2,16,24,12,384]{4,1,3,2,0:T(8,128)} fusion(f32[1,1,16,24,12,384]{5,2,4,3,1,0:T(8,128)} %get-tuple-element.10, f32[1,1,16,24,12,384]{5,2,4,3,1,0:T(8,128)} %get-tuple-element.9), kind=kLoop, calls=%fused_computation | loop fusion | flops 3538944 | bytes 28311552 | tf_op jit(solution)/shard_map/reshape.51
  289.8 29.1 %fusion.22 = f32[2,24,16,12,384]{4,1,3,2,0:T(8,128)} fusion(f32[2,16,24,12,384]{4,1,3,2,0:T(8,128)} %maximum_bitcast_fusion, f32[1,2,24,24]{2,3,0,1:T(8,128)S(1)} %get-tuple-element.68, f32[1,2,24,24]{2,3,0,1:T(8,128)S(1)} %get-tuple-element.67), kind=kOutput, calls=%fused_computation.29 | convolution fusion | flops 2038434048 | bytes 28320768 | tf_op jit(solution)/shard_map/p...kquv,prqm->r...mkuv/dot_general | solution.py:76
  318.9 18.3 %copy.124 = f32[2,24,16,12,384]{4,2,1,3,0:T(8,128)} copy(f32[2,24,16,12,384]{4,1,3,2,0:T(8,128)} %fusion.22) | data formatting | bytes 28311552 | tf_op jit(solution)/shard_map/p...kquv,prqm->r...mkuv/dot_general | solution.py:76
  337.1 13.3 %broadcast_multiply_fusion = f32[2,16,24,12,384]{4,2,1,3,0:T(8,128)} fusion(f32[2,16,24,12,384]{4,2,1,3,0:T(8,128)} %bitcast.260, f32[16,24,12,384]{3,1,0,2:T(8,128)} %bitcast.261), kind=kLoop, calls=%fused_computation.25 | loop fusion | flops 3538944 | bytes 35389440 | tf_op jit(solution)/shard_map/mul | solution.py:137
  350.4 18.3 %fusion.25 = f32[2,16,24,12,384]{4,1,3,2,0:T(8,128)S(1)} fusion(f32[2,16,24,12,384]{4,2,1,3,0:T(8,128)} %broadcast_multiply_fusion, f32[1,2,16,16]{2,3,0,1:T(8,128)S(1)} %get-tuple-element.72, f32[1,2,16,16]{2,3,0,1:T(8,128)S(1)} %get-tuple-element.71), kind=kOutput, calls=%fused_computation.30 | convolution fusion | flops 1358955520 | bytes 28315648 | tf_op jit(solution)/shard_map/p...nquv,prnk->r...kquv/dot_general | solution.py:48
  368.7 6.1 subtract_bitcast_fusion
  374.8 11.7 %maximum_bitcast_fusion.1 = f32[2,16,24,12,384]{4,1,3,2,0:T(8,128)} fusion(f32[1,1,16,24,12,384]{5,2,4,3,1,0:T(8,128)} %get-tuple-element.8, f32[1,1,16,24,12,384]{5,2,4,3,1,0:T(8,128)} %get-tuple-element.7), kind=kLoop, calls=%fused_computation.1 | loop fusion | flops 3538944 | bytes 28311552 | tf_op jit(solution)/shard_map/reshape.67
  386.5 22.1 %fusion.39 = f32[2,12,16,12,384]{4,1,3,2,0:T(8,128)S(1)} fusion(f32[2,16,24,12,384]{4,1,3,2,0:T(8,128)} %maximum_bitcast_fusion.1, f32[1,2,24,12]{2,3,0,1:T(8,128)S(1)} %get-tuple-element.70, f32[1,2,24,12]{2,3,0,1:T(8,128)S(1)} %get-tuple-element.69), kind=kOutput, calls=%fused_computation.54 | convolution fusion | flops 1019217024 | bytes 21238272 | tf_op jit(solution)/shard_map/p...kquv,prqm->r...mkuv/dot_general | solution.py:76
  408.5 6.9 copy.128
  415.4 27.3 %reshape.992 = f32[2,192,12,16,24]{4,3,1,2,0:T(8,128)} reshape(f32[2,12,16,12,384]{4,2,1,3,0:T(8,128)} %copy.128) | data formatting | bytes 14155776 | tf_op jit(solution)/shard_map/reshape.70
  442.7 25.0 %copy.129 = f32[2,192,12,16,24]{1,3,0,4,2:T(8,128)} copy(f32[2,192,12,16,24]{4,3,1,2,0:T(8,128)} %reshape.992) | data formatting | bytes 14155776 | tf_op jit(solution)/shard_map/reshape.70
  467.7 11.4 %fusion.45 = f32[2,1,192,12,16,24]{2,4,5,3,0,1:T(8,128)S(1)} fusion(f32[2,192,12,16,24]{1,3,0,4,2:T(8,128)} %copy.129, f32[1,2,16,16]{2,3,0,1:T(8,128)S(1)} %get-tuple-element.72, f32[1,2,16,16]{2,3,0,1:T(8,128)S(1)} %get-tuple-element.71), kind=kOutput, calls=%fused_computation.56 | convolution fusion | flops 679478272 | bytes 14159872 | tf_op jit(solution)/shard_map/p...nq,prnk->r...kq/dot_general | solution.py:48
  482.7 12.6 %fusion.75 = f32[2,1,192,12,12,16]{2,4,5,3,0,1:T(8,128)S(1)} fusion(f32[2,192,12,16,24]{1,3,4,2,0:T(8,128)S(1)} %maximum_bitcast_fusion.3, f32[1,2,24,12]{2,3,0,1:T(8,128)S(1)} %get-tuple-element.70, f32[1,2,24,12]{2,3,0,1:T(8,128)S(1)} %get-tuple-element.69), kind=kOutput, calls=%fused_computation.98 | convolution fusion | flops 509609088 | bytes 10621440 | tf_op jit(solution)/shard_map/p...kq,prqm->r...mk/dot_general | solution.py:76
  495.3 6.2 copy.131
  501.6 8.2 %copy.132 = f32[2,1,192,12,192]{4,0,3,1,2:T(2,128)} copy(f32[2,1,192,12,192]{2,4,3,0,1:T(8,128)} %bitcast.265) | data formatting | bytes 7077888 | tf_op jit(solution)/shard_map/reshape | solution.py:82
  509.7 4.1 all-to-all-start.1
  514.2 104.7 %all-to-all-done.1 = f32[2,1,192,12,192]{4,0,3,1,2:T(2,128)} async-done(((f32[2,1,192,12,192]{4,0,3,1,2:T(2,128)}), f32[2,1,192,12,192]{4,0,3,1,2:T(2,128)}, u32[]{:S(2)}, u32[]{:S(2)}) %all-to-all-start.1) | async-done | bytes 3538976 | tf_op jit(solution)/shard_map/all_to_all | solution.py:140
  618.9 4.3 copy.133
  623.2 7.0 %fusion.100 = f32[2,1,6,16,24,192]{5,3,4,2,0,1:T(8,128)S(1)} fusion(f32[2,6,16,24,192]{4,0,3,2,1:T(2,128)S(1)} %bitcast.262, f32[1,2,16,16]{2,3,0,1:T(8,128)S(1)} %get-tuple-element.72, f32[1,2,16,16]{2,3,0,1:T(8,128)S(1)} %get-tuple-element.71), kind=kOutput, calls=%fused_computation.131 | convolution fusion | flops 339739648 | bytes 7081984 | tf_op jit(solution)/shard_map/p...nqu,prnk->r...kqu/dot_general | solution.py:48
  631.5 5.9 fusion.103
  642.7 2.3 fusion.183
  645.1 5.3 collective-permute-start.1
  650.9 5.1 collective-permute-done
  658.7 4.7 fusion.52
  669.6 2.2 fusion.58
  672.4 2.9 fusion.198
  675.3 2.2 fusion.197
  677.5 4.5 fusion.67
  689.9 2.9 fusion.181
  (75 shorter events, 34.3 us)
Async XLA Ops:
  24.3 112.7 %all-to-all-start = ((f32[2,1,6,384,192]{4,0,2,1,3:T(2,128)}), f32[2,1,6,384,192]{4,0,2,1,3:T(2,128)}, u32[]{:S(2)}, u32[]{:S(2)}) async-start(f32[2,1,6,384,192]{4,0,2,1,3:T(2,128)} %copy.116), calls=%async_computation | async-start | bytes 9437184 | tf_op jit(solution)/shard_map/all_to_all | solution.py:134
  509.7 109.2 %all-to-all-start.1 = ((f32[2,1,192,12,192]{4,0,3,1,2:T(2,128)}), f32[2,1,192,12,192]{4,0,3,1,2:T(2,128)}, u32[]{:S(2)}, u32[]{:S(2)}) async-start(f32[2,1,192,12,192]{4,0,3,1,2:T(2,128)} %copy.132), calls=%async_computation.1 | async-start | bytes 9437184 | tf_op jit(solution)/shard_map/all_to_all | solution.py:140
  637.8 1.7 copy-start
  638.5 1.9 copy-start.4
  639.4 1.8 copy-start.1
  639.4 2.5 copy-start.2
  639.4 3.2 copy-start.3
  645.0 11.0 %collective-permute-start = (f32[2,1,192,192]{3,2,1,0:T(8,128)S(1)}, f32[2,1,192,192]{3,2,1,0:T(8,128)S(1)}, u32[]{:S(2)}, u32[]{:S(2)}) collective-permute-start(f32[2,1,192,192]{3,2,1,0:T(8,128)S(1)} %get-tuple-element.61), channel_id=1, source_target_pairs={{0,1},{1,2},{2,3},{3,4},{4,5},{5,6},{6,7},{7,8},{8,9},{9,10},{10,1... | collective-permute-start | bytes 884744 | tf_op jit(solution)/shard_map/ppermute | solution.py:21
  645.1 10.9 %collective-permute-start.1 = (f32[2,1,192,192]{3,2,1,0:T(8,128)S(1)}, f32[2,1,192,192]{3,2,1,0:T(8,128)S(1)}, u32[]{:S(2)}, u32[]{:S(2)}) collective-permute-start(f32[2,1,192,192]{3,2,1,0:T(8,128)S(1)} %get-tuple-element.62), channel_id=1, source_target_pairs={{1,0},{2,1},{3,2},{4,3},{5,4},{6,5},{7,6},{8,7},{9,8},{10,9},{11,1... | collective-permute-start | bytes 884744 | tf_op jit(solution)/shard_map/ppermute | solution.py:23
where the time goes:
time: 706 us; the launch traced here: 693 us
  local copies, waits for them, and re-layouts  223 us (32%)
  waiting for transfers between devices  206 us (29%)
  matrix products  156 us (22%)
  other arithmetic  89.4 us (13%)
  starting transfers between devices  17.1 us (2%)
    another operation x6, local copies, waits for them, and re-layouts  129 us
    all_to_all x1, waiting for transfers between devices, on_device(): lax.all_to_all(piece, 'slab', split_axis=2, concat_axis=3, tiled=True)  105 us
    all_to_all x1, waiting for transfers between devices, on_device(): lax.all_to_all(coil_field, 'slab', split_axis=3, concat_axis=2, tiled=True)  96.6 us
    dot_general x6, matrix products, spectral(): jnp.einsum('p...kq' + letters + ',prqm->r...mk' + letters, twisted, compl...  91.3 us
    dot_general x6, matrix products, spectral(): jnp.einsum('p...nq' + letters + ',prnk->r...kq' + letters, parts, complex...  64.2 us
    another operation x6, other arithmetic  27.9 us
    dot_general x2, local copies, waits for them, and re-layouts, spectral(): jnp.einsum('p...kq' + letters + ',prqm->r...mk' + letters, twisted, compl...  25.2 us
    select_n x7, other arithmetic, pair_local(): jnp.where(is_first, (values + after_one) * half_root, (before_one - value...  17.3 us
  transfers between devices with their start and end apart: 4, of which 3 were waited for; matrix products, arithmetic and copies ran while one was open for 1% of the time, Pallas kernels for 0%

commit v1 on v0

v1 whole, which is shorter than its diff:
```python
import functools
import math

import jax
import jax.numpy as jnp
import numpy as np
from jax import lax
from jax.experimental import pallas as pl
from jax.experimental.pallas import tpu as pltpu
from jax.sharding import PartitionSpec as P

half_root = 0.7071067811865476
shrink = 0.5
step_size = 0.25
penalty = 1.0
MESH = pl.DeviceIdType.MESH
f32 = jnp.float32
bf16 = jnp.bfloat16
LANES = 128


def halves(table):
    table = table.astype(np.float32)
    hi = table.astype(bf16)
    lo = (table - hi.astype(np.float32)).astype(bf16)
    return np.stack([hi, lo])


def tables_of(grid_len, width, n, chunks, group, dense):
    cells = np.arange(width)
    freqs = np.arange(grid_len)
    angle = 2.0 * math.pi / grid_len * (np.outer(cells, freqs) % grid_len)
    cos, sin = np.cos(angle), np.sin(angle)
    table_x = np.block([[cos, -sin], [sin, cos]])
    table_z = np.concatenate([cos.T, sin.T])
    table_iz = np.concatenate([cos, sin]) / grid_len
    if not dense:
        by_plane = np.arange(width).reshape(n, -1).T.reshape(-1)
        table_z = table_z[:, by_plane]
        table_iz = np.concatenate([cos[by_plane], sin[by_plane]]) / grid_len
    table_ix = np.block([[cos.T, sin.T], [-sin.T, cos.T]]) / grid_len
    own = chunks * group
    c, j, d = np.meshgrid(np.arange(chunks), np.arange(group), np.arange(n), indexing="ij")
    order = (d * own + c * group + j).reshape(chunks, group * n)
    table_y = np.concatenate([cos.T[order], sin.T[order]], axis=1)
    j, c, s = np.meshgrid(np.arange(group), np.arange(chunks), np.arange(n), indexing="ij")
    order = (s * own + c * group + j).reshape(-1)
    table_iy = np.concatenate([cos[:, order], sin[:, order]]) / grid_len
    return [halves(t) for t in (table_y, table_x, table_z, table_iz, table_ix, table_iy)]


def split(values):
    hi = values.astype(bf16)
    return hi, (values - hi.astype(f32)).astype(bf16)


def mm(a, b):
    return jnp.dot(a, b, preferred_element_type=f32)


def right(values, table):
    hi, lo = split(values)
    return mm(hi, table[0]) + mm(lo, table[0]) + mm(hi, table[1])


def left(table_hi, table_lo, values):
    hi, lo = split(values)
    return mm(table_hi, hi) + mm(table_hi, lo) + mm(table_lo, hi)


def turned(values, sign):
    half = values.shape[-1] // 2
    low, high = values[:, :half], values[:, half:]
    return jnp.concatenate([high * sign, low * -sign], axis=1)


def take(ref, rows):
    return jnp.concatenate([ref[l, rows, :] for l in range(ref.shape[0])], axis=1)


def put(ref, rows, values):
    for l in range(ref.shape[0]):
        ref[l, rows, :] = values[:, l * LANES : (l + 1) * LANES]


def filter_kernel(
    n, planes, chunks, group,
    field, gain_in, ty, tx, tz, tiz, tix, tiy, out,
    send, recv, back, home, gain, wide,
    send_sem, recv_sem, back_sem, home_sem, gain_sem,
):
    me = lax.axis_index("slab")
    width = field.shape[1]
    rows = send.shape[1] // (n * chunks)
    total = n * rows
    if rows == planes * group:
        spans = [(0, n * planes, group)]
    else:
        spans = [(z * group, n, rows) for z in range(planes)]

    gain_copy = pltpu.make_async_copy(gain_in, gain, gain_sem)
    gain_copy.start()
    barrier = pltpu.get_barrier_semaphore()

    def greet(i, carry):
        pl.semaphore_signal(
            barrier, inc=1, device_id={"slab": lax.rem(me + i, n)}, device_id_type=MESH
        )
        return carry

    lax.fori_loop(1, n, greet, 0)

    def push(c, source, target, s_sem, r_sem):
        def one(i, carry):
            to = lax.rem(me + i, n)
            pltpu.make_async_remote_copy(
                src_ref=source.at[:, pl.ds(pl.multiple_of(c * total + to * rows, 8), rows)],
                dst_ref=target.at[:, pl.ds(pl.multiple_of(c * total + me * rows, 8), rows)],
                send_sem=s_sem.at[c],
                recv_sem=r_sem.at[c],
                device_id={"slab": to},
                device_id_type=MESH,
            ).start()
            return carry

        lax.fori_loop(1, n, one, 0)
        own = pl.ds(pl.multiple_of(c * total + me * rows, 8), rows)
        pltpu.make_async_copy(source.at[:, own], target.at[:, own], r_sem.at[c]).start()

    def arrived(c, target, r_sem):
        span = target.at[:, pl.ds(pl.multiple_of(c * total, 8), total)]
        pltpu.make_async_copy(span, span, r_sem.at[c]).wait()

    def left_sent(c, source, s_sem):
        span = source.at[:, pl.ds(pl.multiple_of(c * total, 8), total - rows)]
        pltpu.make_async_copy(span, span, s_sem.at[c]).wait()

    def forward_y(c):
        def plane(z, carry):
            both = left(ty[0, c], ty[1, c], field[z])
            half = group * n
            lines_y = both[:half] + turned(both[half:], 1.0)
            for j in range(group):
                at = pl.ds(c * total + z * group + j, n, stride=rows)
                put(send, at, lines_y[j * n : (j + 1) * n])
            return carry

        lax.fori_loop(0, planes, plane, 0)

    for c in range(chunks):
        forward_y(c)
        if c == 0:
            pl.semaphore_wait(barrier, n - 1)
        push(c, send, recv, send_sem, recv_sem)

    gain_copy.wait()

    def flip(k, carry):
        gain[k] = jnp.transpose(gain[k])
        return carry

    lax.fori_loop(0, chunks * group, flip, 0)

    block = total // 2

    def middle(c, carry):
        arrived(c, recv, recv_sem)

        def forward_x(b, inner):
            at = pl.multiple_of(b * block, 8)
            start = pl.multiple_of(c * total + b * block, 8)
            put(wide, pl.ds(at, block), right(take(recv, pl.ds(start, block)), tx))
            return inner

        lax.fori_loop(0, 2, forward_x, 0)

        def plane(j, inner):
            lines_x = jnp.concatenate(
                [take(wide, pl.ds(j + at, size, stride=step)) for at, size, step in spans], axis=0
            )
            both = left(tz[0], tz[1], lines_x)
            half = both.shape[0] // 2
            spectrum = both[:half] + turned(both[half:], 1.0)
            factor = gain[c * group + j]
            spectrum = spectrum * jnp.concatenate([factor, factor], axis=1)
            both = left(tiz[0], tiz[1], spectrum)
            half = both.shape[0] // 2
            lines_z = both[:half] + turned(both[half:], -1.0)
            for k, (at, size, step) in enumerate(spans):
                put(wide, pl.ds(j + at, size, stride=step), lines_z[k * size : (k + 1) * size])
            return inner

        lax.fori_loop(0, group, plane, 0)

        def inverse_x(b, inner):
            at = pl.multiple_of(b * block, 8)
            start = pl.multiple_of(c * total + b * block, 8)
            put(back, pl.ds(start, block), right(take(wide, pl.ds(at, block)), tix))
            return inner

        lax.fori_loop(0, 2, inverse_x, 0)
        push(c, back, home, back_sem, home_sem)
        return carry

    lax.fori_loop(0, chunks, middle, 0)
    for c in range(chunks):
        arrived(c, home, home_sem)

    def inverse_y(z, carry):
        lines_y = jnp.concatenate(
            [
                take(home, pl.ds(z * group + j, n * chunks, stride=rows))
                for j in range(group)
            ],
            axis=0,
        )
        both = left(tiy[0], tiy[1], lines_y)
        half = both.shape[0] // 2
        out[z] = both[:half] + turned(both[half:], -1.0)
        return carry

    lax.fori_loop(0, planes, inverse_y, 0)
    for c in range(chunks):
        left_sent(c, send, send_sem)
        left_sent(c, back, back_sem)


def filtered(field, kernel, n):
    planes, width, double = field.shape
    own, grid_len, _ = kernel.shape
    fits = [g for g in range(1, own + 1) if own % g == 0 and g * planes % 8 == 0]
    group = fits[0] if fits else own
    chunks = own // group
    rows = -(-planes * group // 8) * 8
    total = n * rows
    tables = tables_of(grid_len, width, n, chunks, group, rows == planes * group)
    vmem = pl.BlockSpec(memory_space=pltpu.VMEM)
    flat = pltpu.VMEM((double // LANES, chunks * total, LANES), f32)
    dma = pltpu.SemaphoreType.DMA
    tables[0] = tables[0].reshape(2, chunks, 2 * group * n, width)
    return pl.pallas_call(
        functools.partial(filter_kernel, n, planes, chunks, group),
        out_shape=jax.ShapeDtypeStruct(field.shape, f32),
        in_specs=[vmem, pl.BlockSpec(memory_space=pl.ANY)] + [vmem] * 6,
        out_specs=vmem,
        scratch_shapes=[
            flat, flat, flat, flat,
            pltpu.VMEM(kernel.shape, f32),
            pltpu.VMEM((2 * grid_len // LANES, total, LANES), f32),
            dma((chunks,)), dma((chunks,)), dma((chunks,)), dma((chunks,)), dma(()),
        ],
        compiler_params=pltpu.CompilerParams(
            collective_id=0, has_side_effects=True, vmem_limit_bytes=60 * 1024 * 1024
        ),
        name="filtered",
    )(field, kernel, *tables)


def pair(values, axis, first):
    length = values.shape[axis]
    after_one = pltpu.roll(values, length - 1, axis)
    before_one = pltpu.roll(values, 1, axis)
    return jnp.where(first, values + after_one, before_one - values)


def blocks(first, second, offset):
    shape = first[0].shape
    row_first = (lax.broadcasted_iota(jnp.int32, shape, 0) + offset) % 2 == 0
    col_first = (lax.broadcasted_iota(jnp.int32, shape, 1) + offset) % 2 == 0
    norm = half_root * half_root * half_root
    sums = [a + b for a, b in zip(first, second)]
    diffs = [a - b for a, b in zip(first, second)]
    result = []
    for which, parts in ((0, sums), (1, diffs)):
        coefs = [pair(pair(p, 0, row_first), 1, col_first) * norm for p in parts]
        magnitude = jnp.sqrt(coefs[0] * coefs[0] + coefs[1] * coefs[1])
        factor = jnp.maximum(magnitude - shrink, 0.0) / jnp.maximum(magnitude, shrink)
        if which == 0:
            factor = jnp.where(row_first & col_first, 1.0, factor)
        result.append(
            [pair(pair(p * factor, 1, col_first), 0, row_first) * norm for p in coefs]
        )
    low = [a + b for a, b in zip(*result)]
    high = [a - b for a, b in zip(*result)]
    return low, high


def spin_kernel(merged, below, above, image_new, dual, prox, dual_new):
    planes = merged.shape[1]

    def read(z):
        return [merged[0, z], merged[1, z]]

    def even(k, carry):
        low, high = blocks(read(2 * k), read(2 * k + 1), 0)
        for part in range(2):
            prox[part, 2 * k] = 0.5 * low[part]
            prox[part, 2 * k + 1] = 0.5 * high[part]
        return carry

    lax.fori_loop(0, planes // 2, even, 0)

    def finish(part, z, value):
        full = prox[part, z] + 0.5 * value
        prox[part, z] = full
        dual_new[part, z] = dual[part, z] + image_new[part, z] - full

    def odd(k, carry):
        low, high = blocks(read(2 * k + 1), read(2 * k + 2), 1)
        for part in range(2):
            finish(part, 2 * k + 1, low[part])
            finish(part, 2 * k + 2, high[part])
        return carry

    lax.fori_loop(0, planes // 2 - 1, odd, 0)
    _, high = blocks([below[0, 0], below[1, 0]], read(0), 1)
    low, _ = blocks(read(planes - 1), [above[0, 0], above[1, 0]], 1)
    for part in range(2):
        finish(part, 0, high[part])
        finish(part, planes - 1, low[part])


def pair_local(values, axis_dim, offset):
    length = values.shape[axis_dim]
    layout = [1] * values.ndim
    layout[axis_dim] = length
    is_first = ((jnp.arange(length) - offset) % 2 == 0).reshape(layout)
    after_one = jnp.roll(values, -1, axis_dim)
    before_one = jnp.roll(values, 1, axis_dim)
    return jnp.where(is_first, (values + after_one) * half_root, (before_one - values) * half_root)


def pair_planes(extended, own_first):
    middle = extended[:, 1:-1]
    after_one = extended[:, 2:]
    before_one = extended[:, :-2]
    marked = own_first[None, :, None, None]
    return jnp.where(marked, (middle + after_one) * half_root, (before_one - middle) * half_root)


def spin(extended, base, offset):
    total_planes = extended.shape[1]
    global_plane = base - 1 + jnp.arange(total_planes, dtype=jnp.int32)
    plane_first = (global_plane - offset) % 2 == 0
    own_first = plane_first[1:-1]
    lower_rim = (extended[:, :1] + extended[:, 1:2]) * half_root
    upper_rim = (extended[:, -2:-1] - extended[:, -1:]) * half_root
    coefs = jnp.concatenate([lower_rim, pair_planes(extended, own_first), upper_rim], axis=1)
    coefs = pair_local(coefs, 2, offset)
    coefs = pair_local(coefs, 3, offset)
    rows_first = (jnp.arange(extended.shape[2]) - offset) % 2 == 0
    cols_first = (jnp.arange(extended.shape[3]) - offset) % 2 == 0
    keep = plane_first[:, None, None] & rows_first[None, :, None] & cols_first[None, None, :]
    magnitude = jnp.sqrt(coefs[0] * coefs[0] + coefs[1] * coefs[1])
    factor = jnp.maximum(magnitude - shrink, 0.0) / jnp.maximum(magnitude, shrink)
    coefs = jnp.where(keep[None], coefs, coefs * factor[None])
    coefs = pair_local(coefs, 3, offset)
    coefs = pair_local(coefs, 2, offset)
    return pair_planes(coefs, own_first)


def on_device(n, image, prox_point, dual, adjoint_data, coil_maps, kernel):
    width = image.shape[3]
    local_real = 0.0
    local_imag = 0.0
    for coil in range(coil_maps.shape[0]):
        sens_real = coil_maps[coil, 0]
        sens_imag = coil_maps[coil, 1]
        field = jnp.concatenate(
            [sens_real * image[0] - sens_imag * image[1], sens_real * image[1] + sens_imag * image[0]],
            axis=-1,
        )
        back = filtered(field, kernel, n)
        back_real, back_imag = back[..., :width], back[..., width:]
        local_real = local_real + (sens_real * back_real + sens_imag * back_imag)
        local_imag = local_imag + (sens_real * back_imag - sens_imag * back_real)
    normal_real, normal_imag = lax.psum((local_real, local_imag), "coil")
    normal = jnp.stack([normal_real, normal_imag])
    image_new = image - step_size * (normal - adjoint_data + penalty * (image - prox_point + dual))
    merged = image_new + dual
    planes = merged.shape[1]
    below = lax.ppermute(merged[:, -1:], "slab", [(i, (i + 1) % n) for i in range(n)])
    above = lax.ppermute(merged[:, :1], "slab", [((i + 1) % n, i) for i in range(n)])
    if planes % 2:
        extended = jnp.concatenate([below, merged, above], axis=1)
        base = lax.axis_index("slab") * planes
        prox_new = 0.5 * (spin(extended, base, 0) + spin(extended, base, 1))
        return (image_new, prox_new, dual + image_new - prox_new)
    vmem = pl.BlockSpec(memory_space=pltpu.VMEM)
    prox_new, dual_new = pl.pallas_call(
        spin_kernel,
        out_shape=[jax.ShapeDtypeStruct(image.shape, f32)] * 2,
        in_specs=[vmem] * 5,
        out_specs=[vmem] * 2,
        compiler_params=pltpu.CompilerParams(vmem_limit_bytes=48 * 1024 * 1024),
        name="spin",
    )(merged, below, above, image_new, dual)
    return (image_new, prox_new, dual_new)


def solution(mesh):
    n = mesh.shape["slab"]
    field = P("recon", "slab", None, None)
    return jax.shard_map(
        functools.partial(on_device, n),
        mesh=mesh,
        in_specs=(field, field, field, field, P("coil", "recon", "slab", None, None), P("slab", None, None)),
        out_specs=(field, field, field),
        check_vma=False,
    )
```

time: 706 us -> 219 us (0.31); the launches traced: 693 us -> 219 us
  local copies, waits for them, and re-layouts: 223 us -> 1.67 us
  waiting for transfers between devices: 206 us -> 10.8 us
  Pallas kernels: 0 us -> 184 us
  matrix products: 156 us -> 0 us
  other arithmetic: 89.4 us -> 9.01 us
    all_to_all x2 -> x0, waiting for transfers between devices: 201 us -> none  [the longest x1 105 us: on_device(): lax.all_to_all(piece, 'slab', split_axis=2, concat_axis=3, tiled=True)]
    pallas_call x0 -> x2, Pallas kernels: none -> 184 us  [the longest x1 161 us: filtered(): pl.pallas_call(functools.partial(filter_kernel, n, planes, chunks, group)...]
    dot_general x12 -> x0, matrix products: 156 us -> none  [the longest x6 91.3 us: spectral(): jnp.einsum('p...kq' + letters + ',prqm->r...mk' + letters, twisted, compl...]
    another operation x8 -> x0, local copies, waits for them, and re-layouts: 130 us -> none
    another operation x12 -> x1, other arithmetic: 40.1 us -> 2.17 us  [on_device(): normal = jnp.stack([normal_real, normal_imag])]
    dot_general x2 -> x0, local copies, waits for them, and re-layouts: 25.2 us -> none  [spectral(): jnp.einsum('p...kq' + letters + ',prqm->r...mk' + letters, twisted, compl...]
    select_n x10 -> x0, other arithmetic: 18.7 us -> none  [the longest x7 17.3 us: pair_local(): jnp.where(is_first, (values + after_one) * half_root, (before_one - value...]
    mul x5 -> x0, other arithmetic: 15.3 us -> none  [the longest x1 13.3 us: on_device(): piece = piece * gain_zyx]
  transfers between devices with their start and end apart: 4 -> 2, of which waited for: 3 -> 2; matrix products, arithmetic and copies ran while one was open for 1% -> 0% of each run, Pallas kernels for 0% -> 0%
where the time goes in v1:
time: 219 us
  Pallas kernels  184 us (84%)
  starting transfers between devices  13 us (6%)
  waiting for transfers between devices  10.8 us (5%)
  other arithmetic  9.01 us (4%)
    pallas_call x1, Pallas kernels, filtered(): pl.pallas_call(functools.partial(filter_kernel, n, planes, chunks, group)...  161 us
    pallas_call x1, Pallas kernels, on_device(): pl.pallas_call(spin_kernel, out_shape=[jax.ShapeDtypeStruct(image.shape,...  22.5 us
    ppermute x1, starting transfers between devices, on_device(): lax.ppermute(merged[:, :1], 'slab', [((i + 1) % n, i) for i in range(n)])  13 us
    ppermute x1, waiting for transfers between devices, on_device(): lax.ppermute(merged[:, -1:], 'slab', [(i, (i + 1) % n) for i in range(n)])  5.5 us
    ppermute x1, waiting for transfers between devices, on_device(): lax.ppermute(merged[:, :1], 'slab', [((i + 1) % n, i) for i in range(n)])  5.29 us
  transfers between devices with their start and end apart: 2, of which 2 were waited for; matrix products, arithmetic and copies ran while one was open for 0% of the time, Pallas kernels for 0%

profile of v1, /device:TPU:0, one launch (start us, length us, event | category | flops | bytes accessed | tf_op | source)
XLA Modules:
  0.0 218.8 jit_solution(4614571956196839722)
XLA Ops:
  0.6 2.6 %fusion.3 = (f32[6,192,192]{2,1,0:T(8,128)S(1)}, f32[6,192,192]{2,1,0:T(8,128)S(1)}) fusion(f32[2,6,192,192]{3,2,1,0:T(8,128)} %param.12, f32[1,2,6,192,192]{4,3,2,1,0:T(8,128)} %param.16), kind=kLoop, calls=%fused_computation.7 | loop fusion | flops 1327104 | bytes 5308416 | tf_op jit(solution)/shard_map/sub | solution.py:370
  3.3 1.6 pad_maximum_fusion.field
  4.9 0.0 copy-start.1
  4.9 161.1 %filtered.1 = f32[6,192,384]{2,1,0:T(8,128)} custom-call(f32[6,192,384]{2,1,0:T(8,128)} %pad_maximum_fusion.field, f32[12,384,384]{2,1,0:T(8,128)} %gain_in.1, bf16[2,3,256,192]{3,2,1,0:T(8,128)(2,1)} %constant.14.clone.ty, bf16[2,384,768]{2,1,0:T(8,128)(2,1)} %constant.15.clone.tx, bf16[2,768,192]{2,1,0:T(8,128)(2,1)} %constant.16.clone.tz, ...), custom_call_target="tpu_custom_call" | custom-call | tf_op jit(solution)/shard_map/filtered/pallas_call | solution.py:241
  165.9 0.0 copy-done.1
  166.0 0.0 copy-start.2
  166.0 0.0 copy-start.3
  166.0 0.0 copy-start.4
  166.0 2.2 fusion.6
  168.2 0.2 copy-done.2
  168.3 0.7 copy-done.3
  169.0 0.7 copy-done.4
  169.8 2.6 %fusion.9 = (f32[2,6,192,192]{3,2,1,0:T(8,128)S(1)}, f32[2,6,192,192]{3,2,1,0:T(8,128)S(1)}) fusion(f32[2,6,192,192]{3,2,1,0:T(8,128)S(1)} %copy-done.3, f32[2,6,192,192]{3,2,1,0:T(8,128)S(1)} %copy-done.2, f32[2,6,192,192]{3,2,1,0:T(8,128)S(1)} %copy-done.4, f32[2,6,192,192]{3,2,1,0:T(8,128)} %param.15, f32[1,6,192,192]{3,2,1,0:T(8,128)S(1)} %get-tuple-element.12, ...), kind=kLoop, calls=%fused_computation.19 | loop fusion | flops 3538944 | bytes 12386304 | tf_op jit(solution)/shard_map/add | solution.py:380
  172.4 0.0 copy-start
  172.4 0.1 fusion.11
  172.5 13.0 %collective-permute-start.1 = (f32[2,1,192,192]{3,2,1,0:T(8,128)S(1)}, f32[2,1,192,192]{3,2,1,0:T(8,128)S(1)}, u32[]{:S(2)}, u32[]{:S(2)}) collective-permute-start(f32[2,1,192,192]{3,2,1,0:T(8,128)S(1)} %get-tuple-element.13), channel_id=1, source_target_pairs={{1,0},{2,1},{3,2},{4,3},{5,4},{6,5},{7,6},{8,7},{9,8},{10,9},{11,1... | collective-permute-start | bytes 884744 | tf_op jit(solution)/shard_map/ppermute | solution.py:383
  185.5 0.0 collective-permute-start
  185.5 5.3 %collective-permute-done.1.above = f32[2,1,192,192]{3,2,1,0:T(8,128)S(1)} collective-permute-done((f32[2,1,192,192]{3,2,1,0:T(8,128)S(1)}, f32[2,1,192,192]{3,2,1,0:T(8,128)S(1)}, u32[]{:S(2)}, u32[]{:S(2)}) %collective-permute-start.1) | collective-permute-done | bytes 294944 | tf_op jit(solution)/shard_map/ppermute | solution.py:383
  190.8 5.5 %collective-permute-done.below = f32[2,1,192,192]{3,2,1,0:T(8,128)S(1)} collective-permute-done((f32[2,1,192,192]{3,2,1,0:T(8,128)S(1)}, f32[2,1,192,192]{3,2,1,0:T(8,128)S(1)}, u32[]{:S(2)}, u32[]{:S(2)}) %collective-permute-start) | collective-permute-done | bytes 294944 | tf_op jit(solution)/shard_map/ppermute | solution.py:382
  196.3 22.5 %spin.1 = (f32[2,6,192,192]{3,2,1,0:T(8,128)}, f32[2,6,192,192]{3,2,1,0:T(8,128)}) custom-call(f32[2,6,192,192]{3,2,1,0:T(8,128)S(1)} %get-tuple-element.7.merged, f32[2,1,192,192]{3,2,1,0:T(8,128)S(1)} %collective-permute-done.below, f32[2,1,192,192]{3,2,1,0:T(8,128)S(1)} %collective-permute-done.1.above, ...), custom_call_target="tpu_custom_call" | custom-call | tf_op jit(solution)/shard_map/spin/pallas_call | solution.py:390
  218.8 0.0 copy-done
Async XLA Ops:
  4.9 161.1 %copy-start.1 = (f32[1,2,6,192,192]{4,3,2,1,0:T(8,128)S(1)}, f32[1,2,6,192,192]{4,3,2,1,0:T(8,128)}, u32[]{:S(2)}) copy-start(f32[1,2,6,192,192]{4,3,2,1,0:T(8,128)} %param.16) | copy-start | bytes 5308420
  166.0 2.4 %copy-start.2 = (f32[2,6,192,192]{3,2,1,0:T(8,128)S(1)}, f32[2,6,192,192]{3,2,1,0:T(8,128)}, u32[]{:S(2)}) copy-start(f32[2,6,192,192]{3,2,1,0:T(8,128)} %param.12) | copy-start | bytes 5308420
  166.0 3.1 %copy-start.3 = (f32[2,6,192,192]{3,2,1,0:T(8,128)S(1)}, f32[2,6,192,192]{3,2,1,0:T(8,128)}, u32[]{:S(2)}) copy-start(f32[2,6,192,192]{3,2,1,0:T(8,128)} %dual.1) | copy-start | bytes 5308420
  166.0 3.8 %copy-start.4 = (f32[2,6,192,192]{3,2,1,0:T(8,128)S(1)}, f32[2,6,192,192]{3,2,1,0:T(8,128)}, u32[]{:S(2)}) copy-start(f32[2,6,192,192]{3,2,1,0:T(8,128)} %param.13) | copy-start | bytes 5308420
  172.4 46.4 %copy-start = (f32[2,6,192,192]{3,2,1,0:T(8,128)}, f32[2,6,192,192]{3,2,1,0:T(8,128)S(1)}, u32[]{:S(2)}) copy-start(f32[2,6,192,192]{3,2,1,0:T(8,128)S(1)} %get-tuple-element.8.image_new) | copy-start | bytes 5308420
  172.5 18.3 %collective-permute-start.1 = (f32[2,1,192,192]{3,2,1,0:T(8,128)S(1)}, f32[2,1,192,192]{3,2,1,0:T(8,128)S(1)}, u32[]{:S(2)}, u32[]{:S(2)}) collective-permute-start(f32[2,1,192,192]{3,2,1,0:T(8,128)S(1)} %get-tuple-element.13), channel_id=1, source_target_pairs={{1,0},{2,1},{3,2},{4,3},{5,4},{6,5},{7,6},{8,7},{9,8},{10,9},{11,1... | collective-permute-start | bytes 884744 | tf_op jit(solution)/shard_map/ppermute | solution.py:383
  185.5 10.8 %collective-permute-start = (f32[2,1,192,192]{3,2,1,0:T(8,128)S(1)}, f32[2,1,192,192]{3,2,1,0:T(8,128)S(1)}, u32[]{:S(2)}, u32[]{:S(2)}) collective-permute-start(f32[2,1,192,192]{3,2,1,0:T(8,128)S(1)} %get-tuple-element.14), channel_id=1, source_target_pairs={{0,1},{1,2},{2,3},{3,4},{4,5},{5,6},{6,7},{7,8},{8,9},{9,10},{10,1... | collective-permute-start | bytes 884744 | tf_op jit(solution)/shard_map/ppermute | solution.py:382

commit v2 on v1

--- a/solution.py
+++ b/solution.py
@@ -83,14 +83,163 @@
         ref[l, rows, :] = values[:, l * LANES : (l + 1) * LANES]
 
 
-def filter_kernel(
+def filter_kernel(n, planes, chunks, group, field, gain_in, ty, tx, tz, tiz, tix, tiy, out, *scratch):
+    def finish(z, value):
+        out[z] = value
+
+    def inverse(plane):
+        lax.fori_loop(0, planes, plane, 0)
+
+    filter_body(
+        n, planes, chunks, group, lambda z: field[z], finish, (lambda: None, lambda: None), inverse,
+        gain_in, ty, tx, tz, tiz, tix, tiy, *scratch,
+    )
+
+
+def spin_pair(mg, px, table, edge, first, second, offset, add):
+    count = edge // 2
+
+    def rows(plane, odd):
+        return pl.ds(plane * edge + odd, count, stride=2)
+
+    def lines(plane):
+        even, odd = take(mg, rows(plane, 0)), take(mg, rows(plane, 1))
+        return (odd, pltpu.roll(even, count - 1, 0)) if offset else (even, odd)
+
+    (f0, s0), (f1, s1) = lines(first), lines(second)
+    uf, us, vf, vs = f0 + f1, s0 + s1, f0 - f1, s0 - s1
+    cells = jnp.concatenate([uf + us, uf - us, vf + vs, vf - vs], axis=0)
+
+    def along_x(values):
+        hi, lo = split(values)
+        return mm(hi, table[offset]) + mm(lo, table[offset])
+
+    coefs = along_x(cells)
+    squares = coefs * coefs
+    half = squares.shape[1] // 2
+    squares = squares + jnp.concatenate([squares[:, half:], squares[:, :half]], axis=1)
+    factor = 1.0 - lax.rsqrt(jnp.maximum(0.5 * squares, 1.0))
+    row = lax.broadcasted_iota(jnp.int32, factor.shape, 0)
+    col = lax.broadcasted_iota(jnp.int32, factor.shape, 1)
+    factor = jnp.where((row < count) & ((col + offset) % 2 == 0), 1.0, factor)
+    cells = along_x(coefs * factor) * 0.0625
+    uf, us, vf, vs = (cells[k * count : (k + 1) * count] for k in range(4))
+    uf, us, vf, vs = uf + us, uf - us, vf + vs, vf - vs
+    for plane, f, s in ((first, uf + vf, us + vs), (second, uf - vf, us - vs)):
+        even, odd = (pltpu.roll(s, 1, 0), f) if offset else (f, s)
+        if add:
+            even = even + take(px, rows(plane, 0))
+            odd = odd + take(px, rows(plane, 1))
+        put(px, rows(plane, 0), even)
+        put(px, rows(plane, 1), odd)
+
+
+def step_kernel(
     n, planes, chunks, group,
-    field, gain_in, ty, tx, tz, tiz, tix, tiy, out,
+    image, coil, late_a, late_b, late_c, gain_in, ty,
+    ltx, ltz, ltiz, ltix, ltiy, lpx,
+    image_new, prox_new, dual_new,
+    prox_point, dual, adjoint, tx, tz, tiz, tix, tiy, table, mg, px,
+    late_sem, halo_out, halo_in, *scratch,
+):
+    me = lax.axis_index("slab")
+    edge, width = image.shape[2:]
+    pairs = [
+        (ltx, tx), (ltz, tz), (ltiz, tiz), (ltix, tix), (ltiy, tiy), (lpx, table),
+        (late_a, prox_point), (late_b, dual), (late_c, adjoint),
+    ]
+    copies = [pltpu.make_async_copy(a, b, late_sem.at[k]) for k, (a, b) in enumerate(pairs)]
+
+    def begin():
+        for copy in copies:
+            copy.start()
+
+    def ready():
+        for copy in copies:
+            copy.wait()
+
+    def field(z):
+        sr, si, re, im = coil[0, z], coil[1, z], image[0, z], image[1, z]
+        return jnp.concatenate([sr * re - si * im, sr * im + si * re], axis=1)
+
+    def finish(z, value):
+        back = (value[:, :width], value[:, width:])
+        sr, si = coil[0, z], coil[1, z]
+        normal = (sr * back[0] + si * back[1], sr * back[1] - si * back[0])
+        merged = []
+        for part in range(2):
+            old, point, scaled = image[part, z], prox_point[part, z], dual[part, z]
+            new = old - step_size * (normal[part] - adjoint[part, z] + penalty * (old - point + scaled))
+            image_new[part, z] = new
+            merged.append(new + scaled)
+        put(mg, pl.ds((z + 1) * edge, edge), jnp.concatenate(merged, axis=1))
+
+    def span(plane):
+        return mg.at[:, pl.ds(plane * edge, edge)]
+
+    up = pltpu.make_async_remote_copy(
+        src_ref=span(planes), dst_ref=span(0), send_sem=halo_out.at[0], recv_sem=halo_in.at[0],
+        device_id={"slab": lax.rem(me + 1, n)}, device_id_type=MESH,
+    )
+    down = pltpu.make_async_remote_copy(
+        src_ref=span(1), dst_ref=span(planes + 1), send_sem=halo_out.at[1], recv_sem=halo_in.at[1],
+        device_id={"slab": lax.rem(me + n - 1, n)}, device_id_type=MESH,
+    )
+
+    def inverse(plane):
+        def rim(k, carry):
+            return plane(k * (planes - 1), carry)
+
+        lax.fori_loop(0, 2, rim, 0)
+        up.start()
+        down.start()
+        lax.fori_loop(1, planes - 1, plane, 0)
+
+    filter_body(
+        n, planes, chunks, group, field, finish, (begin, ready), inverse,
+        gain_in, ty, tx, tz, tiz, tix, tiy, *scratch,
+    )
+
+    for plane in (0, planes + 1):
+        put(px, pl.ds(plane * edge, edge), jnp.zeros((edge, 2 * width), f32))
+
+    def even(k, carry):
+        spin_pair(mg, px, table, edge, 2 * k + 1, 2 * k + 2, 0, False)
+        return carry
+
+    def odd(k, carry):
+        spin_pair(mg, px, table, edge, 2 * k, 2 * k + 1, 1, True)
+        return carry
+
+    def rim(k, carry):
+        return odd(k * (planes // 2), carry)
+
+    def close(z, carry):
+        at = pl.ds((z + 1) * edge, edge)
+        prox = take(px, at)
+        scaled = take(mg, at) - prox
+        for part in range(2):
+            prox_new[part, z] = prox[:, part * width : (part + 1) * width]
+            dual_new[part, z] = scaled[:, part * width : (part + 1) * width]
+        return carry
+
+    lax.fori_loop(0, planes // 2, even, 0)
+    lax.fori_loop(1, planes // 2, odd, 0)
+    lax.fori_loop(1, planes - 1, close, 0)
+    up.wait()
+    down.wait()
+    lax.fori_loop(0, 2, rim, 0)
+    lax.fori_loop(0, 2, lambda k, carry: close(k * (planes - 1), carry), 0)
+
+
+def filter_body(
+    n, planes, chunks, group, field, finish, late, inverse,
+    gain_in, ty, tx, tz, tiz, tix, tiy,
     send, recv, back, home, gain, wide,
     send_sem, recv_sem, back_sem, home_sem, gain_sem,
 ):
+    begin, ready = late
     me = lax.axis_index("slab")
-    width = field.shape[1]
     rows = send.shape[1] // (n * chunks)
     total = n * rows
     if rows == planes * group:
@@ -109,6 +258,7 @@
         return carry
 
     lax.fori_loop(1, n, greet, 0)
+    begin()
 
     def push(c, source, target, s_sem, r_sem):
         def one(i, carry):
@@ -137,7 +287,7 @@
 
     def forward_y(c):
         def plane(z, carry):
-            both = left(ty[0, c], ty[1, c], field[z])
+            both = left(ty[0, c], ty[1, c], field(z))
             half = group * n
             lines_y = both[:half] + turned(both[half:], 1.0)
             for j in range(group):
@@ -154,6 +304,7 @@
         push(c, send, recv, send_sem, recv_sem)
 
     gain_copy.wait()
+    ready()
 
     def flip(k, carry):
         gain[k] = jnp.transpose(gain[k])
@@ -216,17 +367,17 @@
         )
         both = left(tiy[0], tiy[1], lines_y)
         half = both.shape[0] // 2
-        out[z] = both[:half] + turned(both[half:], -1.0)
-        return carry
-
-    lax.fori_loop(0, planes, inverse_y, 0)
+        finish(z, both[:half] + turned(both[half:], -1.0))
+        return carry
+
+    inverse(inverse_y)
     for c in range(chunks):
         left_sent(c, send, send_sem)
         left_sent(c, back, back_sem)
 
 
-def filtered(field, kernel, n):
-    planes, width, double = field.shape
+def plan(shape, kernel, n):
+    planes, width, double = shape
     own, grid_len, _ = kernel.shape
     fits = [g for g in range(1, own + 1) if own % g == 0 and g * planes % 8 == 0]
     group = fits[0] if fits else own
@@ -234,21 +385,59 @@
     rows = -(-planes * group // 8) * 8
     total = n * rows
     tables = tables_of(grid_len, width, n, chunks, group, rows == planes * group)
-    vmem = pl.BlockSpec(memory_space=pltpu.VMEM)
     flat = pltpu.VMEM((double // LANES, chunks * total, LANES), f32)
     dma = pltpu.SemaphoreType.DMA
     tables[0] = tables[0].reshape(2, chunks, 2 * group * n, width)
+    scratch = [
+        flat, flat, flat, flat,
+        pltpu.VMEM(kernel.shape, f32),
+        pltpu.VMEM((2 * grid_len // LANES, total, LANES), f32),
+        dma((chunks,)), dma((chunks,)), dma((chunks,)), dma((chunks,)), dma(()),
+    ]
+    return chunks, group, tables, scratch
+
+
+def fused(image, prox_point, dual, adjoint, coil, kernel, n):
+    _, planes, edge, width = image.shape
+    chunks, group, tables, scratch = plan((planes, edge, 2 * width), kernel, n)
+    haar = np.zeros((2, 2 * width, 2 * width), np.float32)
+    for offset in range(2):
+        for part in range(2):
+            first = (np.arange(width // 2) * 2 + offset) % width + part * width
+            second = (np.arange(width // 2) * 2 + offset + 1) % width + part * width
+            haar[offset, first, first] = haar[offset, first, second] = 1.0
+            haar[offset, second, first] = 1.0
+            haar[offset, second, second] = -1.0
+    tables.append(haar.astype(bf16))
+    vmem = pl.BlockSpec(memory_space=pltpu.VMEM)
+    apart = pl.BlockSpec(memory_space=pl.ANY)
+    held = [pltpu.VMEM(image.shape, f32)] * 3
+    held += [pltpu.VMEM(t.shape, bf16) for t in tables[1:]]
+    lines = pltpu.VMEM((2 * width // LANES, (planes + 2) * edge, LANES), f32)
+    dma = pltpu.SemaphoreType.DMA
+    return pl.pallas_call(
+        functools.partial(step_kernel, n, planes, chunks, group),
+        out_shape=[jax.ShapeDtypeStruct(image.shape, f32)] * 3,
+        in_specs=[vmem, vmem] + [apart] * 4 + [vmem] + [apart] * 6,
+        out_specs=[vmem] * 3,
+        scratch_shapes=held + [lines, lines, dma((9,)), dma((2,)), dma((2,))] + scratch,
+        compiler_params=pltpu.CompilerParams(
+            collective_id=0, has_side_effects=True, vmem_limit_bytes=67043328
+        ),
+        name="fused",
+    )(image, coil, prox_point, dual, adjoint, kernel, *tables)
+
+
+def filtered(field, kernel, n):
+    planes = field.shape[0]
+    chunks, group, tables, scratch = plan(field.shape, kernel, n)
+    vmem = pl.BlockSpec(memory_space=pltpu.VMEM)
     return pl.pallas_call(
         functools.partial(filter_kernel, n, planes, chunks, group),
         out_shape=jax.ShapeDtypeStruct(field.shape, f32),
         in_specs=[vmem, pl.BlockSpec(memory_space=pl.ANY)] + [vmem] * 6,
         out_specs=vmem,
-        scratch_shapes=[
-            flat, flat, flat, flat,
-            pltpu.VMEM(kernel.shape, f32),
-            pltpu.VMEM((2 * grid_len // LANES, total, LANES), f32),
-            dma((chunks,)), dma((chunks,)), dma((chunks,)), dma((chunks,)), dma(()),
-        ],
+        scratch_shapes=scratch,
         compiler_params=pltpu.CompilerParams(
             collective_id=0, has_side_effects=True, vmem_limit_bytes=60 * 1024 * 1024
         ),
@@ -359,8 +548,10 @@
     return pair_planes(coefs, own_first)
 
 
-def on_device(n, image, prox_point, dual, adjoint_data, coil_maps, kernel):
+def on_device(n, coils, image, prox_point, dual, adjoint_data, coil_maps, kernel):
     width = image.shape[3]
+    if coils == 1 and coil_maps.shape[0] == 1 and image.shape[1] % 2 == 0:
+        return tuple(fused(image, prox_point, dual, adjoint_data, coil_maps[0], kernel, n))
     local_real = 0.0
     local_imag = 0.0
     for coil in range(coil_maps.shape[0]):
@@ -402,7 +593,7 @@
     n = mesh.shape["slab"]
     field = P("recon", "slab", None, None)
     return jax.shard_map(
-        functools.partial(on_device, n),
+        functools.partial(on_device, n, mesh.shape["coil"]),
         mesh=mesh,
         in_specs=(field, field, field, field, P("coil", "recon", "slab", None, None), P("slab", None, None)),
         out_specs=(field, field, field),

time: 219 us -> 191 us (0.87)
  starting transfers between devices: 13 us -> 0 us
  waiting for transfers between devices: 10.8 us -> 0 us
  other arithmetic: 9.01 us -> 0 us
  local copies, waits for them, and re-layouts: 1.67 us -> 7.3 us
    ppermute x2 -> x0, starting transfers between devices: 13 us -> none  [the longest x1 13 us: on_device(): lax.ppermute(merged[:, :1], 'slab', [((i + 1) % n, i) for i in range(n)])]
    ppermute x2 -> x0, waiting for transfers between devices: 10.8 us -> none  [the longest x1 5.5 us: on_device(): lax.ppermute(merged[:, -1:], 'slab', [(i, (i + 1) % n) for i in range(n)])]
    unnamed x10 -> x7, local copies, waits for them, and re-layouts: 1.62 us -> 7.3 us
    sub x1 -> x0, other arithmetic: 2.65 us -> none  [on_device(): sens_real * image[0] - sens_imag * image[1]]
    add x1 -> x0, other arithmetic: 2.61 us -> none  [on_device(): merged = image_new + dual]
    pallas_call x2 -> x1, Pallas kernels: 184 us -> 182 us  [fused(): pl.pallas_call(functools.partial(step_kernel, n, planes, chunks, group),...]
  transfers between devices with their start and end apart: 2 -> 0, of which waited for: 2 -> 0; matrix products, arithmetic and copies ran while one was open for 0% -> 0% of each run, Pallas kernels for 0% -> 0%
where the time goes in v2:
time: 191 us; the launch traced here: 190 us
  Pallas kernels  182 us (95%)
  local copies, waits for them, and re-layouts  7.3 us (4%)
    pallas_call x1, Pallas kernels, fused(): pl.pallas_call(functools.partial(step_kernel, n, planes, chunks, group),...  182 us
    unnamed x7, local copies, waits for them, and re-layouts  7.3 us

profile of v2, /device:TPU:0, one launch (start us, length us, event | category | flops | bytes accessed | tf_op | source)
XLA Modules:
  0.0 190.4 jit_solution(12529278709899829965)
XLA Ops:
  0.6 182.5 %fused.1 = (f32[2,6,192,192]{3,2,1,0:T(8,128)}, f32[2,6,192,192]{3,2,1,0:T(8,128)}, f32[2,6,192,192]{3,2,1,0:T(8,128)}) custom-call(f32[2,6,192,192]{3,2,1,0:T(8,128)} %image.1, f32[2,6,192,192]{3,2,1,0:T(8,128)} %bitcast.1, f32[2,6,192,192]{3,2,1,0:T(8,128)} %late_a.1, f32[2,6,192,192]{3,2,1,0:T(8,128)} %late_b.1, f32[2,6,192,192]{3,2,1,0:T(8,128)} %late_c.1, ...), custom_call_target="tpu_custom_call" | custom-call | tf_op jit(solution)/shard_map/fused/pallas_call | solution.py:418
  183.1 0.0 copy-start.1
  183.1 3.4 %copy.19 = f32[2,6,192,192]{3,2,1,0:T(8,128)} copy(f32[2,6,192,192]{3,2,1,0:T(8,128)} %get-tuple-element.6) | data formatting | bytes 3538944
  186.5 0.0 copy-done.1
  186.5 0.0 copy-start
  186.5 1.4 copy.20
  187.9 1.1 copy-done
  189.0 1.4 copy.21
Async XLA Ops:
  183.1 3.4 %copy-start.1 = (f32[2,6,192,192]{3,2,1,0:T(8,128)S(1)}, f32[2,6,192,192]{3,2,1,0:T(8,128)}, u32[]{:S(2)}) copy-start(f32[2,6,192,192]{3,2,1,0:T(8,128)} %get-tuple-element.7) | copy-start | bytes 5308420
  186.5 2.5 %copy-start = (f32[2,6,192,192]{3,2,1,0:T(8,128)S(1)}, f32[2,6,192,192]{3,2,1,0:T(8,128)}, u32[]{:S(2)}) copy-start(f32[2,6,192,192]{3,2,1,0:T(8,128)} %get-tuple-element.8) | copy-start | bytes 5308420

commit v3 on v2

--- a/solution.py
+++ b/solution.py
@@ -43,9 +43,10 @@
     c, j, d = np.meshgrid(np.arange(chunks), np.arange(group), np.arange(n), indexing="ij")
     order = (d * own + c * group + j).reshape(chunks, group * n)
     table_y = np.concatenate([cos.T[order], sin.T[order]], axis=1)
-    j, c, s = np.meshgrid(np.arange(group), np.arange(chunks), np.arange(n), indexing="ij")
-    order = (s * own + c * group + j).reshape(-1)
-    table_iy = np.concatenate([cos[:, order], sin[:, order]]) / grid_len
+    c, j, s = np.meshgrid(np.arange(chunks), np.arange(group), np.arange(n), indexing="ij")
+    order = (s * own + c * group + j).reshape(chunks, 1, -1)
+    both = np.concatenate([cos, sin])[:, :] / grid_len
+    table_iy = np.stack([both[:, order[c, 0]] for c in range(chunks)])
     return [halves(t) for t in (table_y, table_x, table_z, table_iz, table_ix, table_iy)]
 
 
@@ -138,9 +139,9 @@
     n, planes, chunks, group,
     image, coil, late_a, late_b, late_c, gain_in, ty,
     ltx, ltz, ltiz, ltix, ltiy, lpx,
-    image_new, prox_new, dual_new,
-    prox_point, dual, adjoint, tx, tz, tiz, tix, tiy, table, mg, px,
-    late_sem, halo_out, halo_in, *scratch,
+    image_out, prox_out, dual_out,
+    image_new, prox_new, dual_new, prox_point, dual, adjoint, tx, tz, tiz, tix, tiy, table, mg, px,
+    late_sem, halo_out, halo_in, out_sem, *scratch,
 ):
     me = lax.axis_index("slab")
     edge, width = image.shape[2:]
@@ -200,6 +201,17 @@
         gain_in, ty, tx, tz, tiz, tix, tiy, *scratch,
     )
 
+    written = [pltpu.make_async_copy(image_new, image_out, out_sem.at[0])]
+    written[0].start()
+
+    def write(k, start, size):
+        for buffer, whole in ((prox_new, prox_out), (dual_new, dual_out)):
+            part = pl.ds(start, size)
+            copy = pltpu.make_async_copy(buffer.at[:, part], whole.at[:, part], out_sem.at[k])
+            copy.start()
+            written.append(copy)
+            k += 1
+
     for plane in (0, planes + 1):
         put(px, pl.ds(plane * edge, edge), jnp.zeros((edge, 2 * width), f32))
 
@@ -225,11 +237,17 @@
 
     lax.fori_loop(0, planes // 2, even, 0)
     lax.fori_loop(1, planes // 2, odd, 0)
-    lax.fori_loop(1, planes - 1, close, 0)
+    if planes > 2:
+        lax.fori_loop(1, planes - 1, close, 0)
+        write(1, 1, planes - 2)
     up.wait()
     down.wait()
     lax.fori_loop(0, 2, rim, 0)
     lax.fori_loop(0, 2, lambda k, carry: close(k * (planes - 1), carry), 0)
+    write(3, 0, 1)
+    write(5, planes - 1, 1)
+    for copy in written:
+        copy.wait()
 
 
 def filter_body(
@@ -355,24 +373,35 @@
 
     lax.fori_loop(0, chunks, middle, 0)
     for c in range(chunks):
+        left_sent(c, send, send_sem)
+
+    def inverse_y(c, z):
+        lines_y = jnp.concatenate(
+            [take(home, pl.ds(c * total + z * group + j, n, stride=rows)) for j in range(group)], axis=0
+        )
+        both = left(tiy[0, c], tiy[1, c], lines_y)
+        half = both.shape[0] // 2
+        value = both[:half] + turned(both[half:], -1.0)
+        if c:
+            value = value + take(send, pl.ds(z * half, half))
+        if c < chunks - 1:
+            put(send, pl.ds(z * half, half), value)
+        else:
+            finish(z, value)
+
+    def over(c):
+        def plane(z, carry):
+            inverse_y(c, z)
+            return carry
+
+        return plane
+
+    for c in range(chunks):
         arrived(c, home, home_sem)
-
-    def inverse_y(z, carry):
-        lines_y = jnp.concatenate(
-            [
-                take(home, pl.ds(z * group + j, n * chunks, stride=rows))
-                for j in range(group)
-            ],
-            axis=0,
-        )
-        both = left(tiy[0], tiy[1], lines_y)
-        half = both.shape[0] // 2
-        finish(z, both[:half] + turned(both[half:], -1.0))
-        return carry
-
-    inverse(inverse_y)
+        if c < chunks - 1:
+            lax.fori_loop(0, planes, over(c), 0)
+    inverse(over(chunks - 1))
     for c in range(chunks):
-        left_sent(c, send, send_sem)
         left_sent(c, back, back_sem)
 
 
@@ -411,7 +440,7 @@
     tables.append(haar.astype(bf16))
     vmem = pl.BlockSpec(memory_space=pltpu.VMEM)
     apart = pl.BlockSpec(memory_space=pl.ANY)
-    held = [pltpu.VMEM(image.shape, f32)] * 3
+    held = [pltpu.VMEM(image.shape, f32)] * 6
     held += [pltpu.VMEM(t.shape, bf16) for t in tables[1:]]
     lines = pltpu.VMEM((2 * width // LANES, (planes + 2) * edge, LANES), f32)
     dma = pltpu.SemaphoreType.DMA
@@ -419,8 +448,8 @@
         functools.partial(step_kernel, n, planes, chunks, group),
         out_shape=[jax.ShapeDtypeStruct(image.shape, f32)] * 3,
         in_specs=[vmem, vmem] + [apart] * 4 + [vmem] + [apart] * 6,
-        out_specs=[vmem] * 3,
-        scratch_shapes=held + [lines, lines, dma((9,)), dma((2,)), dma((2,))] + scratch,
+        out_specs=[apart] * 3,
+        scratch_shapes=held + [lines, lines, dma((9,)), dma((2,)), dma((2,)), dma((7,))] + scratch,
         compiler_params=pltpu.CompilerParams(
             collective_id=0, has_side_effects=True, vmem_limit_bytes=67043328
         ),

time: 191 us -> 188 us (0.984)
  Pallas kernels: 182 us -> 180 us
    pallas_call x1, Pallas kernels: 182 us -> 180 us  [fused(): pl.pallas_call(functools.partial(step_kernel, n, planes, chunks, group),...]
where the time goes in v3:
time: 188 us
  Pallas kernels  180 us (96%)
  local copies, waits for them, and re-layouts  7.3 us (4%)
    pallas_call x1, Pallas kernels, fused(): pl.pallas_call(functools.partial(step_kernel, n, planes, chunks, group),...  180 us
    unnamed x7, local copies, waits for them, and re-layouts  7.3 us

profile of v3, /device:TPU:0, one launch (start us, length us, event | category | flops | bytes accessed | tf_op | source)
XLA Modules:
  0.0 187.9 jit_solution(1179590886195450640)
XLA Ops:
  0.6 179.9 %fused.1 = (f32[2,6,192,192]{3,2,1,0:T(8,128)}, f32[2,6,192,192]{3,2,1,0:T(8,128)}, f32[2,6,192,192]{3,2,1,0:T(8,128)}) custom-call(f32[2,6,192,192]{3,2,1,0:T(8,128)} %image.1, f32[2,6,192,192]{3,2,1,0:T(8,128)} %bitcast.1, f32[2,6,192,192]{3,2,1,0:T(8,128)} %late_a.1, f32[2,6,192,192]{3,2,1,0:T(8,128)} %late_b.1, f32[2,6,192,192]{3,2,1,0:T(8,128)} %late_c.1, ...), custom_call_target="tpu_custom_call" | custom-call | tf_op jit(solution)/shard_map/fused/pallas_call | solution.py:447
  180.6 0.0 copy-start.1
  180.6 3.4 %copy.19 = f32[2,6,192,192]{3,2,1,0:T(8,128)} copy(f32[2,6,192,192]{3,2,1,0:T(8,128)} %get-tuple-element.6) | data formatting | bytes 3538944
  183.9 0.0 copy-done.1
  184.0 0.0 copy-start
  184.0 1.4 copy.20
  185.4 1.1 copy-done
  186.5 1.4 copy.21
Async XLA Ops:
  180.6 3.4 %copy-start.1 = (f32[2,6,192,192]{3,2,1,0:T(8,128)S(1)}, f32[2,6,192,192]{3,2,1,0:T(8,128)}, u32[]{:S(2)}) copy-start(f32[2,6,192,192]{3,2,1,0:T(8,128)} %get-tuple-element.7) | copy-start | bytes 5308420
  184.0 2.5 %copy-start = (f32[2,6,192,192]{3,2,1,0:T(8,128)S(1)}, f32[2,6,192,192]{3,2,1,0:T(8,128)}, u32[]{:S(2)}) copy-start(f32[2,6,192,192]{3,2,1,0:T(8,128)} %get-tuple-element.8) | copy-start | bytes 5308420

commit v4 on v3

--- a/solution.py
+++ b/solution.py
@@ -280,7 +280,8 @@
 
     def push(c, source, target, s_sem, r_sem):
         def one(i, carry):
-            to = lax.rem(me + i, n)
+            far = n // 2 + (i // 2) * (2 * (i % 2) - 1)
+            to = lax.rem(me + far, n)
             pltpu.make_async_remote_copy(
                 src_ref=source.at[:, pl.ds(pl.multiple_of(c * total + to * rows, 8), rows)],
                 dst_ref=target.at[:, pl.ds(pl.multiple_of(c * total + me * rows, 8), rows)],

time: 188 us -> 186 us (0.989)
  Pallas kernels: 180 us -> 177 us
    pallas_call x1, Pallas kernels: 180 us -> 177 us  [fused(): pl.pallas_call(functools.partial(step_kernel, n, planes, chunks, group),...]
where the time goes in v4:
time: 186 us; the launch traced here: 185 us
  Pallas kernels  177 us (95%)
  local copies, waits for them, and re-layouts  7.3 us (4%)
    pallas_call x1, Pallas kernels, fused(): pl.pallas_call(functools.partial(step_kernel, n, planes, chunks, group),...  177 us
    unnamed x7, local copies, waits for them, and re-layouts  7.3 us

profile of v4, /device:TPU:0, one launch (start us, length us, event | category | flops | bytes accessed | tf_op | source)
XLA Modules:
  0.0 185.4 jit_solution(2371759384331180358)
XLA Ops:
  0.6 177.4 %fused.1 = (f32[2,6,192,192]{3,2,1,0:T(8,128)}, f32[2,6,192,192]{3,2,1,0:T(8,128)}, f32[2,6,192,192]{3,2,1,0:T(8,128)}) custom-call(f32[2,6,192,192]{3,2,1,0:T(8,128)} %image.1, f32[2,6,192,192]{3,2,1,0:T(8,128)} %bitcast.1, f32[2,6,192,192]{3,2,1,0:T(8,128)} %late_a.1, f32[2,6,192,192]{3,2,1,0:T(8,128)} %late_b.1, f32[2,6,192,192]{3,2,1,0:T(8,128)} %late_c.1, ...), custom_call_target="tpu_custom_call" | custom-call | tf_op jit(solution)/shard_map/fused/pallas_call | solution.py:448
  178.1 0.0 copy-start.1
  178.1 3.4 %copy.19 = f32[2,6,192,192]{3,2,1,0:T(8,128)} copy(f32[2,6,192,192]{3,2,1,0:T(8,128)} %get-tuple-element.6) | data formatting | bytes 3538944
  181.4 0.0 copy-done.1
  181.4 0.0 copy-start
  181.4 1.4 copy.20
  182.9 1.1 copy-done
  184.0 1.4 copy.21
Async XLA Ops:
  178.1 3.4 %copy-start.1 = (f32[2,6,192,192]{3,2,1,0:T(8,128)S(1)}, f32[2,6,192,192]{3,2,1,0:T(8,128)}, u32[]{:S(2)}) copy-start(f32[2,6,192,192]{3,2,1,0:T(8,128)} %get-tuple-element.7) | copy-start | bytes 5308420
  181.4 2.5 %copy-start = (f32[2,6,192,192]{3,2,1,0:T(8,128)S(1)}, f32[2,6,192,192]{3,2,1,0:T(8,128)}, u32[]{:S(2)}) copy-start(f32[2,6,192,192]{3,2,1,0:T(8,128)} %get-tuple-element.8) | copy-start | bytes 5308420
